TPU v7x, 512 devices: a whole 4x4x16 slice. The times are simulated.
512 devices in a mesh: leaf: 128 (over z, y, core), level: 4 (over x).
Axes of the slice: x: 4, y: 4, z: 16, core: 2. Of those that a mesh axis runs over, the one named last changes fastest.
Arguments:
- points_x: bfloat16 [256, 262144], P(None, ('leaf', 'level')), may hold values from -6 to 6
- leaf_basis: bfloat16 [512, 512, 256], P(('leaf', 'level')), may hold values from -0.25 to 0.25
- near_tiles: bfloat16 [512, 4, 512, 512], P(('leaf', 'level')), may hold values from -0.25 to 0.25
- near_cols: int32 [512, 4], P(('leaf', 'level')), may hold values from 0 to 11, as said below
- near_count: int32 [512], P(('leaf', 'level')), may hold values from 3 to 4, as said below
- transfer: bfloat16 [2, 256, 256], replicated, may hold values from -0.3125 to 0.3125
- coupling: bfloat16 [6, 2, 256, 256], replicated, may hold values from -0.375 to 0.375
- couple_mask: int32 [6, 128, 2], replicated, may hold values 0 or 1
Outputs:
- kernel_product: bfloat16 [256, 262144], P(None, ('leaf', 'level'))
Inputs may be any that keep to these rules, and one draw needn't show every extreme that they name: Slots 0, 1 and 2 of leaf L name L itself, L - 1 and L + 1 (near_cols 4 + L mod 4, one less, one more); slot 3 names any leaf of the previous, own or next group; some leaf's slot 3 names 0 and some names 11. The live slots of a leaf are its first near_count slots; in every draw some leaf has 3 and some has 4 live slots.
All inputs are finite; a program needn't handle non-finite values.
Results may differ from a plain program's by a relative error of at most 0.015.
Values may be sent and summed in bfloat16 or wider, within the bound.
A program may use at most 64 MiB of HBM per device.

v0:
```python
from functools import partial
import jax
import jax.numpy as jnp
from jax import lax
from jax.sharding import PartitionSpec as P


def shifted(value, axis, steps):
    count = lax.axis_size(axis)
    leading, last = (max(0, -steps), min(count, count - steps))
    return lax.ppermute(value, axis, [(source, source + steps) for source in range(leading, last)])


def with_halo(block, sides, width):
    for axis, dim in sides:
        count = lax.axis_size(axis)
        forward = [(i, i + 1) for i in range(count - 1)]
        backward = [(target, source) for source, target in forward]
        low = lax.ppermute(
            lax.slice_in_dim(block, block.shape[dim] - width, None, axis=dim), axis, forward
        )
        high = lax.ppermute(lax.slice_in_dim(block, 0, width, axis=dim), axis, backward)
        block = jnp.concatenate([low, block, high], axis=dim)
    return block


def in_one_piece(arrays, axis, dim, along):
    widths = [a.shape[along] for a in arrays]
    both = jnp.concatenate(arrays, axis=along)
    whole = lax.all_gather(both, axis, axis=dim, tiled=True)
    return tuple(jnp.split(whole, [sum(widths[:k]) for k in range(1, len(widths))], axis=along))


def swapped(block, axis, distance):
    count = lax.axis_size(axis)
    route = []
    for low in range(count):
        high = low | 1 << distance
        if high != low and high < count:
            route += [(low, high), (high, low)]
    return lax.ppermute(block, axis, route)


def pair_sum(lower_coef, upper_coef, transfer):
    summed = jnp.dot(lower_coef, transfer[0], preferred_element_type=jnp.float32)
    summed = summed + jnp.dot(upper_coef, transfer[1], preferred_element_type=jnp.float32)
    return summed.astype(jnp.bfloat16)


def down_one(fields, matrix):
    return lax.dot_general(
        fields, matrix, (((1,), (1,)), ((), ())), preferred_element_type=jnp.float32
    )


def partner(coefs, distance):
    return shifted(coefs, "leaf", distance)


def add_tile(column_x, tile_block, running):
    return running + jnp.dot(column_x, tile_block, preferred_element_type=jnp.float32)


def keep_same(running):
    return running


def per_device(
    points_x, leaf_basis, near_tiles, near_cols, near_count, transfer, coupling, couple_mask
):
    group_size = lax.axis_size("level")
    leaf_count = lax.axis_size("leaf")
    group_pos = lax.axis_index("level")
    leaf_pos = lax.axis_index("leaf")
    vectors, points = points_x.shape
    leaf_map = leaf_basis[0]
    slot_count = near_tiles.shape[1]
    levels = coupling.shape[0]
    group_bits = group_size.bit_length() - 1
    leaf_bits = leaf_count.bit_length() - 1
    active = min(levels, leaf_bits + 1)
    leaf_coef = jnp.dot(points_x, leaf_map, preferred_element_type=jnp.float32).astype(jnp.bfloat16)
    padded = with_halo(points_x, (("leaf", 1),), points)
    left_g, own_g, right_g, group_coef = (
        *in_one_piece((padded[:, :points], points_x, padded[:, 2 * points :]), "level", 1, 0),
        lax.all_gather(leaf_coef[None], "level", axis=0, tiled=True),
    )
    window_x = jnp.concatenate([left_g, own_g, right_g], axis=1)
    level_coefs = [group_coef[member] for member in range(group_size)]
    while len(level_coefs) > 1:
        level_coefs = [
            pair_sum(level_coefs[2 * pair_idx], level_coefs[2 * pair_idx + 1], transfer)
            for pair_idx in range(len(level_coefs) // 2)
        ]
    top_coef = level_coefs[0]
    vec_share = vectors // group_size
    top_coef = lax.dynamic_slice_in_dim(top_coef, group_pos * vec_share, vec_share, 0)
    coarse = [top_coef]
    for level_idx in range(1, active):
        bit_num = level_idx - 1
        current = coarse[-1]
        own_side = leaf_pos >> bit_num & 1
        is_upper = own_side == 1
        partner_coef = swapped(current, "leaf", bit_num)
        lower_coef = jnp.where(is_upper, partner_coef, current)
        upper_coef = jnp.where(is_upper, current, partner_coef)
        coarse.append(pair_sum(lower_coef, upper_coef, transfer))
    couplings = []
    for level_idx in range(active):
        stride = 1 << level_idx
        cluster = leaf_pos >> level_idx
        coupled = jnp.zeros(coarse[level_idx].shape, jnp.float32)
        for pick_idx, offset in enumerate((2, 3)):
            matrix = coupling[level_idx, pick_idx]
            ahead_coef = partner(coarse[level_idx], -offset * stride)
            behind = partner(coarse[level_idx], offset * stride)
            ahead_mask = couple_mask[level_idx, cluster, pick_idx].astype(jnp.float32)
            behind_mask = couple_mask[level_idx, jnp.maximum(cluster - offset, 0), pick_idx].astype(
                jnp.float32
            )
            coupled = coupled + ahead_mask * jnp.dot(
                ahead_coef, matrix, preferred_element_type=jnp.float32
            )
            coupled = coupled + behind_mask * down_one(behind, matrix)
        couplings.append(coupled)
    fields = couplings[active - 1].astype(jnp.bfloat16)
    for level_idx in range(active - 2, -1, -1):
        child_side = leaf_pos >> level_idx & 1
        fields = (down_one(fields, transfer[child_side]) + couplings[level_idx]).astype(
            jnp.bfloat16
        )
    fields = lax.all_gather(fields, "level", axis=0, tiled=True)
    for bit_num in range(group_bits - 1, -1, -1):
        child_side = group_pos >> bit_num & 1
        fields = down_one(fields, transfer[child_side]).astype(jnp.bfloat16)
    far_field = down_one(fields, leaf_map)
    tile_count = near_count[0]
    near_field = far_field
    for slot_idx in range(slot_count):
        column_x = lax.dynamic_slice_in_dim(window_x, near_cols[0, slot_idx] * points, points, 1)
        near_field = lax.cond(
            slot_idx < tile_count,
            partial(add_tile, column_x, near_tiles[0, slot_idx]),
            keep_same,
            near_field,
        )
    return near_field.astype(jnp.bfloat16)


def solution(mesh):
    in_specs = (
        P(None, ("leaf", "level")),
        P(("leaf", "level"), None, None),
        P(("leaf", "level"), None, None, None),
        P(("leaf", "level"), None),
        P(("leaf", "level")),
        P(),
        P(),
        P(),
    )
    out_specs = P(None, ("leaf", "level"))
    return jax.shard_map(
        per_device, mesh=mesh, in_specs=in_specs, out_specs=out_specs, check_vma=False
    )
```

profile of v0, /device:TPU:2, one launch (start us, length us, event | category | flops | bytes accessed | tf_op | source)
XLA Modules:
  0.0 276.6 jit_solution(5910400586805205190)
XLA Ops:
  6.5 2.6 collective-permute-start.29
  9.1 1.3 collective-permute-start.30
  10.4 1.2 convolution_convert_fusion
  11.6 15.7 %all-gather = bf16[1024,256]{1,0:T(8,128)(2,1)S(1)} all-gather(bf16[256,256]{1,0:T(8,128)(2,1)S(1)} %convolution_convert_fusion), channel_id=2, replica_groups=mesh['leaf'=128,'level'=4] {'level'}, dimensions={0}, use_global_device_ids=true | all-gather | bytes 655360 | tf_op jit(solution)/shard_map/all_gather | solution.py:86
  27.3 1.1 fusion.64
  29.3 1.3 collective-permute-start.27
  30.6 3.2 %collective-permute-start.26 = (bf16[64,256]{1,0:T(8,128)(2,1)S(1)}, bf16[64,256]{1,0:T(8,128)(2,1)S(1)}, u32[]{:S(2)}, u32[]{:S(2)}) collective-permute-start(bf16[64,256]{1,0:T(8,128)(2,1)S(1)} %fusion.166), channel_id=1, source_target_pairs={{0,8},{4,12},{8,16},{12,20},{16,24},{20,28},{24,32},{28,36},{32,40... | collective-permute-start | bytes 98312 | tf_op jit(solution)/shard_map/ppermute | solution.py:11
  33.8 3.1 %collective-permute-start = (bf16[64,256]{1,0:T(8,128)(2,1)S(1)}, bf16[64,256]{1,0:T(8,128)(2,1)S(1)}, u32[]{:S(2)}, u32[]{:S(2)}) collective-permute-start(bf16[64,256]{1,0:T(8,128)(2,1)S(1)} %fusion.166), channel_id=1, source_target_pairs={{0,4},{4,0},{8,12},{12,8},{16,20},{20,16},{24,28},{28,24},{32,36},... | collective-permute-start | bytes 98312 | tf_op jit(solution)/shard_map/ppermute | solution.py:41
  55.8 1.3 collective-permute-start.25
  57.5 3.9 %collective-permute-start.28 = (bf16[64,256]{1,0:T(8,128)(2,1)S(1)}, bf16[64,256]{1,0:T(8,128)(2,1)S(1)}, u32[]{:S(2)}, u32[]{:S(2)}) collective-permute-start(bf16[64,256]{1,0:T(8,128)(2,1)S(1)} %fusion.166), channel_id=1, source_target_pairs={{0,12},{4,16},{8,20},{12,24},{16,28},{20,32},{24,36},{28,40},{32,4... | collective-permute-start | bytes 98312 | tf_op jit(solution)/shard_map/ppermute | solution.py:11
  61.5 8.9 %collective-permute-start.24 = (bf16[64,256]{1,0:T(8,128)(2,1)S(1)}, bf16[64,256]{1,0:T(8,128)(2,1)S(1)}, u32[]{:S(2)}, u32[]{:S(2)}) collective-permute-start(bf16[64,256]{1,0:T(8,128)(2,1)S(1)} %fusion.44), channel_id=1, source_target_pairs={{0,24},{4,28},{8,32},{12,36},{16,40},{20,44},{24,48},{28,52},{32,5... | collective-permute-start | bytes 98312 | tf_op jit(solution)/shard_map/ppermute | solution.py:11
  70.6 1.9 collective-permute-start.1
  72.7 3.7 %collective-permute-done.1 = bf16[64,256]{1,0:T(8,128)(2,1)S(1)} collective-permute-done((bf16[64,256]{1,0:T(8,128)(2,1)S(1)}, bf16[64,256]{1,0:T(8,128)(2,1)S(1)}, u32[]{:S(2)}, u32[]{:S(2)}) %collective-permute-start.1) | collective-permute-done | bytes 32800 | tf_op jit(solution)/shard_map/ppermute | solution.py:41
  76.4 1.3 collective-permute-start.23
  78.0 1.4 collective-permute-start.22
  79.6 3.9 %collective-permute-done.23 = bf16[64,256]{1,0:T(8,128)(2,1)S(1)} collective-permute-done((bf16[64,256]{1,0:T(8,128)(2,1)S(1)}, bf16[64,256]{1,0:T(8,128)(2,1)S(1)}, u32[]{:S(2)}, u32[]{:S(2)}) %collective-permute-start.23) | collective-permute-done | bytes 32800 | tf_op jit(solution)/shard_map/ppermute | solution.py:11
  83.4 1.3 collective-permute-start.21
  84.9 6.1 %collective-permute-start.2 = (bf16[64,256]{1,0:T(8,128)(2,1)S(1)}, bf16[64,256]{1,0:T(8,128)(2,1)S(1)}, u32[]{:S(2)}, u32[]{:S(2)}) collective-permute-start(bf16[64,256]{1,0:T(8,128)(2,1)S(1)} %fusion.45), channel_id=1, source_target_pairs={{0,16},{16,0},{4,20},{20,4},{8,24},{24,8},{12,28},{28,12},{32,48},... | collective-permute-start | bytes 98312 | tf_op jit(solution)/shard_map/ppermute | solution.py:41
  91.1 1.7 collective-permute-done.2
  92.8 6.8 %collective-permute-start.20 = (bf16[64,256]{1,0:T(8,128)(2,1)S(1)}, bf16[64,256]{1,0:T(8,128)(2,1)S(1)}, u32[]{:S(2)}, u32[]{:S(2)}) collective-permute-start(bf16[64,256]{1,0:T(8,128)(2,1)S(1)} %fusion.45), channel_id=1, source_target_pairs={{0,48},{4,52},{8,56},{12,60},{16,64},{20,68},{24,72},{28,76},{32,8... | collective-permute-start | bytes 98312 | tf_op jit(solution)/shard_map/ppermute | solution.py:11
  99.8 1.4 collective-permute-done.20
  101.2 1.3 collective-permute-start.19
  102.6 10.0 %collective-permute-done.19 = bf16[64,256]{1,0:T(8,128)(2,1)S(1)} collective-permute-done((bf16[64,256]{1,0:T(8,128)(2,1)S(1)}, bf16[64,256]{1,0:T(8,128)(2,1)S(1)}, u32[]{:S(2)}, u32[]{:S(2)}) %collective-permute-start.19) | collective-permute-done | bytes 32800 | tf_op jit(solution)/shard_map/ppermute | solution.py:11
  112.7 5.8 %collective-permute-start.18 = (bf16[64,256]{1,0:T(8,128)(2,1)S(1)}, bf16[64,256]{1,0:T(8,128)(2,1)S(1)}, u32[]{:S(2)}, u32[]{:S(2)}) collective-permute-start(bf16[64,256]{1,0:T(8,128)(2,1)S(1)} %fusion.45), channel_id=1, source_target_pairs={{0,32},{4,36},{8,40},{12,44},{16,48},{20,52},{24,56},{28,60},{32,6... | collective-permute-start | bytes 98312 | tf_op jit(solution)/shard_map/ppermute | solution.py:11
  118.6 1.4 collective-permute-done.18
  120.0 1.3 collective-permute-start.17
  121.7 10.8 %collective-permute-start.16 = (bf16[64,256]{1,0:T(8,128)(2,1)S(1)}, bf16[64,256]{1,0:T(8,128)(2,1)S(1)}, u32[]{:S(2)}, u32[]{:S(2)}) collective-permute-start(bf16[64,256]{1,0:T(8,128)(2,1)S(1)} %fusion.46), channel_id=1, source_target_pairs={{0,96},{4,100},{8,104},{12,108},{16,112},{20,116},{24,120},{28,124... | collective-permute-start | bytes 98312 | tf_op jit(solution)/shard_map/ppermute | solution.py:11
  132.5 5.4 %collective-permute-start.3 = (bf16[64,256]{1,0:T(8,128)(2,1)S(1)}, bf16[64,256]{1,0:T(8,128)(2,1)S(1)}, u32[]{:S(2)}, u32[]{:S(2)}) collective-permute-start(bf16[64,256]{1,0:T(8,128)(2,1)S(1)} %fusion.46), channel_id=1, source_target_pairs={{0,32},{32,0},{4,36},{36,4},{8,40},{40,8},{12,44},{44,12},{16,48},... | collective-permute-start | bytes 98312 | tf_op jit(solution)/shard_map/ppermute | solution.py:41
  138.0 2.0 pad_maximum_fusion.1
  140.0 1.3 collective-permute-start.15
  141.6 5.2 %collective-permute-start.14 = (bf16[64,256]{1,0:T(8,128)(2,1)S(1)}, bf16[64,256]{1,0:T(8,128)(2,1)S(1)}, u32[]{:S(2)}, u32[]{:S(2)}) collective-permute-start(bf16[64,256]{1,0:T(8,128)(2,1)S(1)} %fusion.46), channel_id=1, source_target_pairs={{0,64},{4,68},{8,72},{12,76},{16,80},{20,84},{24,88},{28,92},{32,9... | collective-permute-start | bytes 98312 | tf_op jit(solution)/shard_map/ppermute | solution.py:11
  147.6 1.3 collective-permute-start.13
  149.0 7.8 %collective-permute-start.4 = (bf16[64,256]{1,0:T(8,128)(2,1)S(1)}, bf16[64,256]{1,0:T(8,128)(2,1)S(1)}, u32[]{:S(2)}, u32[]{:S(2)}) collective-permute-start(bf16[64,256]{1,0:T(8,128)(2,1)S(1)} %fusion.47), channel_id=1, source_target_pairs={{0,64},{64,0},{4,68},{68,4},{8,72},{72,8},{12,76},{76,12},{16,80},... | collective-permute-start | bytes 98312 | tf_op jit(solution)/shard_map/ppermute | solution.py:41
  157.0 2.1 collective-permute-done.4
  159.0 10.5 %collective-permute-start.12 = (bf16[64,256]{1,0:T(8,128)(2,1)S(1)}, bf16[64,256]{1,0:T(8,128)(2,1)S(1)}, u32[]{:S(2)}, u32[]{:S(2)}) collective-permute-start(bf16[64,256]{1,0:T(8,128)(2,1)S(1)} %fusion.47), channel_id=1, source_target_pairs={{0,192},{4,196},{8,200},{12,204},{16,208},{20,212},{24,216},{28,22... | collective-permute-start | bytes 98312 | tf_op jit(solution)/shard_map/ppermute | solution.py:11
  169.9 1.3 collective-permute-done.12
  171.1 1.3 collective-permute-start.11
  172.6 10.4 %collective-permute-done.11 = bf16[64,256]{1,0:T(8,128)(2,1)S(1)} collective-permute-done((bf16[64,256]{1,0:T(8,128)(2,1)S(1)}, bf16[64,256]{1,0:T(8,128)(2,1)S(1)}, u32[]{:S(2)}, u32[]{:S(2)}) %collective-permute-start.11) | collective-permute-done | bytes 32800 | tf_op jit(solution)/shard_map/ppermute | solution.py:11
  182.9 5.2 %collective-permute-start.10 = (bf16[64,256]{1,0:T(8,128)(2,1)S(1)}, bf16[64,256]{1,0:T(8,128)(2,1)S(1)}, u32[]{:S(2)}, u32[]{:S(2)}) collective-permute-start(bf16[64,256]{1,0:T(8,128)(2,1)S(1)} %fusion.47), channel_id=1, source_target_pairs={{0,128},{4,132},{8,136},{12,140},{16,144},{20,148},{24,152},{28,15... | collective-permute-start | bytes 98312 | tf_op jit(solution)/shard_map/ppermute | solution.py:11
  188.3 1.4 collective-permute-done.10
  189.7 12.0 %collective-permute-start.8 = (bf16[64,256]{1,0:T(8,128)(2,1)S(1)}, bf16[64,256]{1,0:T(8,128)(2,1)S(1)}, u32[]{:S(2)}, u32[]{:S(2)}) collective-permute-start(bf16[64,256]{1,0:T(8,128)(2,1)S(1)} %fusion.48), channel_id=1, source_target_pairs={{0,384},{4,388},{8,392},{12,396},{16,400},{20,404},{24,408},{28,41... | collective-permute-start | bytes 98312 | tf_op jit(solution)/shard_map/ppermute | solution.py:11
  201.9 1.4 collective-permute-done.8
  203.3 1.3 collective-permute-start.7
  204.7 8.3 %collective-permute-done.7 = bf16[64,256]{1,0:T(8,128)(2,1)S(1)} collective-permute-done((bf16[64,256]{1,0:T(8,128)(2,1)S(1)}, bf16[64,256]{1,0:T(8,128)(2,1)S(1)}, u32[]{:S(2)}, u32[]{:S(2)}) %collective-permute-start.7) | collective-permute-done | bytes 32800 | tf_op jit(solution)/shard_map/ppermute | solution.py:11
  213.0 1.3 collective-permute-start.6
  214.4 1.4 collective-permute-done.6
  215.9 1.3 collective-permute-start.5
  217.3 13.1 %collective-permute-done.5 = bf16[64,256]{1,0:T(8,128)(2,1)S(1)} collective-permute-done((bf16[64,256]{1,0:T(8,128)(2,1)S(1)}, bf16[64,256]{1,0:T(8,128)(2,1)S(1)}, u32[]{:S(2)}, u32[]{:S(2)}) %collective-permute-start.5) | collective-permute-done | bytes 32800 | tf_op jit(solution)/shard_map/ppermute | solution.py:11
  230.4 1.3 collective-permute-start.9
  232.7 7.6 %collective-permute-done.9 = bf16[64,256]{1,0:T(8,128)(2,1)} collective-permute-done((bf16[64,256]{1,0:T(8,128)(2,1)S(1)}, bf16[64,256]{1,0:T(8,128)(2,1)}, u32[]{:S(2)}, u32[]{:S(2)}) %collective-permute-start.9) | collective-permute-done | bytes 32800 | tf_op jit(solution)/shard_map/ppermute | solution.py:11
  241.4 1.0 fusion.57
  242.4 1.0 fusion.58
  243.5 1.0 fusion.59
  244.7 12.0 %all_gather.10 = bf16[256,256]{1,0:T(8,128)(2,1)S(1)} all-gather(bf16[64,256]{1,0:T(8,128)(2,1)S(1)} %fusion.49), channel_id=1, replica_groups=mesh['leaf'=128,'level'=4] {'level'}, dimensions={0}, use_global_device_ids=true | all-gather | bytes 163840 | tf_op jit(solution)/shard_map/all_gather | solution.py:132
  257.4 2.2 fusion.217
  259.7 1.8 pad_maximum_fusion
  262.4 1.3 conditional.7
  262.4 1.3 convolution_add_fusion.1
  263.7 1.4 conditional.8
  263.7 1.3 convolution_add_fusion.2
  265.1 1.4 conditional.9
  265.1 1.3 convolution_add_fusion.3
  266.4 2.5 conditional.11
  267.7 1.3 convolution_add_fusion
  (76 shorter events, 12.6 us)
Async XLA Ops:
  6.5 3.9 %copy-start = (bf16[1,512,256]{2,1,0:T(8,128)(2,1)S(1)}, bf16[1,512,256]{2,1,0:T(8,128)(2,1)}, u32[]{:S(2)}) copy-start(bf16[1,512,256]{2,1,0:T(8,128)(2,1)} %param.17) | copy-start | bytes 786436
  6.5 21.8 %copy-start.1 = (bf16[2,256,256]{2,1,0:T(8,128)(2,1)S(1)}, bf16[2,256,256]{2,1,0:T(8,128)(2,1)}, u32[]{:S(2)}) copy-start(bf16[2,256,256]{2,1,0:T(8,128)(2,1)} %param.21) | copy-start | bytes 786436
  6.5 250.8 %all-gather.3.cloned.1.call-start = ((), (), s32[]{:S(2)}) async-start(), calls=%async_computation | async-start | bytes 3932160 | tf_op jit(solution)/shard_map/all_gather | solution.py:30
  6.5 115.1 %collective-permute-start.29 = (bf16[256,512]{1,0:T(8,128)(2,1)}, bf16[256,512]{1,0:T(8,128)(2,1)}, u32[]{:S(2)}, u32[]{:S(2)}) collective-permute-start(bf16[256,512]{1,0:T(8,128)(2,1)} %param.16), channel_id=1, source_target_pairs={{0,4},{4,8},{8,12},{12,16},{16,20},{20,24},{24,28},{28,32},{32,36}... | collective-permute-start | bytes 786440 | tf_op jit(solution)/shard_map/ppermute | solution.py:19
  9.1 123.4 %collective-permute-start.30 = (bf16[256,512]{1,0:T(8,128)(2,1)}, bf16[256,512]{1,0:T(8,128)(2,1)}, u32[]{:S(2)}, u32[]{:S(2)}) collective-permute-start(bf16[256,512]{1,0:T(8,128)(2,1)} %param.16), channel_id=1, source_target_pairs={{4,0},{8,4},{12,8},{16,12},{20,16},{24,20},{28,24},{32,28},{36,32}... | collective-permute-start | bytes 786440 | tf_op jit(solution)/shard_map/ppermute | solution.py:22
  27.3 9.6 %copy-start.7 = (s32[1,4]{1,0:T(1,128)S(1)}, s32[1,4]{1,0:T(1,128)}, u32[]{:S(2)}) copy-start(s32[1,4]{1,0:T(1,128)} %param.19) | copy-start | bytes 52
  27.3 12.8 %copy-start.6 = (s32[6,128,2]{1,2,0:T(2,128)S(1)}, s32[6,128,2]{1,2,0:T(2,128)}, u32[]{:S(2)}) copy-start(s32[6,128,2]{1,2,0:T(2,128)} %param.23) | copy-start | bytes 18436
  28.6 32.8 %copy-start.2 = (bf16[6,2,256,256]{3,2,1,0:T(8,128)(2,1)S(1)}, bf16[6,2,256,256]{3,2,1,0:T(8,128)(2,1)}, u32[]{:S(2)}) copy-start(bf16[6,2,256,256]{3,2,1,0:T(8,128)(2,1)} %param.22) | copy-start | bytes 4718596
  29.3 28.2 %collective-permute-start.27 = (bf16[64,256]{1,0:T(8,128)(2,1)S(1)}, bf16[64,256]{1,0:T(8,128)(2,1)S(1)}, u32[]{:S(2)}, u32[]{:S(2)}) collective-permute-start(bf16[64,256]{1,0:T(8,128)(2,1)S(1)} %fusion.166), channel_id=1, source_target_pairs={{12,0},{16,4},{20,8},{24,12},{28,16},{32,20},{36,24},{40,28},{44,3... | collective-permute-start | bytes 98312 | tf_op jit(solution)/shard_map/ppermute | solution.py:11
  30.6 30.9 %collective-permute-start.26 = (bf16[64,256]{1,0:T(8,128)(2,1)S(1)}, bf16[64,256]{1,0:T(8,128)(2,1)S(1)}, u32[]{:S(2)}, u32[]{:S(2)}) collective-permute-start(bf16[64,256]{1,0:T(8,128)(2,1)S(1)} %fusion.166), channel_id=1, source_target_pairs={{0,8},{4,12},{8,16},{12,20},{16,24},{20,28},{24,32},{28,36},{32,40... | collective-permute-start | bytes 98312 | tf_op jit(solution)/shard_map/ppermute | solution.py:11
  33.8 22.0 %collective-permute-start = (bf16[64,256]{1,0:T(8,128)(2,1)S(1)}, bf16[64,256]{1,0:T(8,128)(2,1)S(1)}, u32[]{:S(2)}, u32[]{:S(2)}) collective-permute-start(bf16[64,256]{1,0:T(8,128)(2,1)S(1)} %fusion.166), channel_id=1, source_target_pairs={{0,4},{4,0},{8,12},{12,8},{16,20},{20,16},{24,28},{28,24},{32,36},... | collective-permute-start | bytes 98312 | tf_op jit(solution)/shard_map/ppermute | solution.py:41
  55.8 188.7 %collective-permute-start.25 = (bf16[64,256]{1,0:T(8,128)(2,1)S(1)}, bf16[64,256]{1,0:T(8,128)(2,1)S(1)}, u32[]{:S(2)}, u32[]{:S(2)}) collective-permute-start(bf16[64,256]{1,0:T(8,128)(2,1)S(1)} %fusion.166), channel_id=1, source_target_pairs={{8,0},{12,4},{16,8},{20,12},{24,16},{28,20},{32,24},{36,28},{40,32... | collective-permute-start | bytes 98312 | tf_op jit(solution)/shard_map/ppermute | solution.py:11
  57.5 13.2 %collective-permute-start.28 = (bf16[64,256]{1,0:T(8,128)(2,1)S(1)}, bf16[64,256]{1,0:T(8,128)(2,1)S(1)}, u32[]{:S(2)}, u32[]{:S(2)}) collective-permute-start(bf16[64,256]{1,0:T(8,128)(2,1)S(1)} %fusion.166), channel_id=1, source_target_pairs={{0,12},{4,16},{8,20},{12,24},{16,28},{20,32},{24,36},{28,40},{32,4... | collective-permute-start | bytes 98312 | tf_op jit(solution)/shard_map/ppermute | solution.py:11
  61.4 76.6 %copy-start.4 = (bf16[256,512]{1,0:T(8,128)(2,1)S(1)}, bf16[256,512]{1,0:T(8,128)(2,1)}, u32[]{:S(2)}) copy-start(bf16[256,512]{1,0:T(8,128)(2,1)} %param.16) | copy-start | bytes 786436
  61.5 16.5 %collective-permute-start.24 = (bf16[64,256]{1,0:T(8,128)(2,1)S(1)}, bf16[64,256]{1,0:T(8,128)(2,1)S(1)}, u32[]{:S(2)}, u32[]{:S(2)}) collective-permute-start(bf16[64,256]{1,0:T(8,128)(2,1)S(1)} %fusion.44), channel_id=1, source_target_pairs={{0,24},{4,28},{8,32},{12,36},{16,40},{20,44},{24,48},{28,52},{32,5... | collective-permute-start | bytes 98312 | tf_op jit(solution)/shard_map/ppermute | solution.py:11
  70.6 5.8 %collective-permute-start.1 = (bf16[64,256]{1,0:T(8,128)(2,1)S(1)}, bf16[64,256]{1,0:T(8,128)(2,1)S(1)}, u32[]{:S(2)}, u32[]{:S(2)}) collective-permute-start(bf16[64,256]{1,0:T(8,128)(2,1)S(1)} %fusion.44), channel_id=1, source_target_pairs={{0,8},{8,0},{4,12},{12,4},{16,24},{24,16},{20,28},{28,20},{32,40},... | collective-permute-start | bytes 98312 | tf_op jit(solution)/shard_map/ppermute | solution.py:41
  76.4 7.0 %collective-permute-start.23 = (bf16[64,256]{1,0:T(8,128)(2,1)S(1)}, bf16[64,256]{1,0:T(8,128)(2,1)S(1)}, u32[]{:S(2)}, u32[]{:S(2)}) collective-permute-start(bf16[64,256]{1,0:T(8,128)(2,1)S(1)} %fusion.44), channel_id=1, source_target_pairs={{24,0},{28,4},{32,8},{36,12},{40,16},{44,20},{48,24},{52,28},{56,3... | collective-permute-start | bytes 98312 | tf_op jit(solution)/shard_map/ppermute | solution.py:11
  78.0 6.8 %collective-permute-start.22 = (bf16[64,256]{1,0:T(8,128)(2,1)S(1)}, bf16[64,256]{1,0:T(8,128)(2,1)S(1)}, u32[]{:S(2)}, u32[]{:S(2)}) collective-permute-start(bf16[64,256]{1,0:T(8,128)(2,1)S(1)} %fusion.44), channel_id=1, source_target_pairs={{0,16},{4,20},{8,24},{12,28},{16,32},{20,36},{24,40},{28,44},{32,4... | collective-permute-start | bytes 98312 | tf_op jit(solution)/shard_map/ppermute | solution.py:11
  83.4 160.0 %collective-permute-start.21 = (bf16[64,256]{1,0:T(8,128)(2,1)S(1)}, bf16[64,256]{1,0:T(8,128)(2,1)}, u32[]{:S(2)}, u32[]{:S(2)}) collective-permute-start(bf16[64,256]{1,0:T(8,128)(2,1)S(1)} %fusion.44), channel_id=1, source_target_pairs={{16,0},{20,4},{24,8},{28,12},{32,16},{36,20},{40,24},{44,28},{48,3... | collective-permute-start | bytes 98312 | tf_op jit(solution)/shard_map/ppermute | solution.py:11
  84.9 7.9 %collective-permute-start.2 = (bf16[64,256]{1,0:T(8,128)(2,1)S(1)}, bf16[64,256]{1,0:T(8,128)(2,1)S(1)}, u32[]{:S(2)}, u32[]{:S(2)}) collective-permute-start(bf16[64,256]{1,0:T(8,128)(2,1)S(1)} %fusion.45), channel_id=1, source_target_pairs={{0,16},{16,0},{4,20},{20,4},{8,24},{24,8},{12,28},{28,12},{32,48},... | collective-permute-start | bytes 98312 | tf_op jit(solution)/shard_map/ppermute | solution.py:41
  92.8 8.4 %collective-permute-start.20 = (bf16[64,256]{1,0:T(8,128)(2,1)S(1)}, bf16[64,256]{1,0:T(8,128)(2,1)S(1)}, u32[]{:S(2)}, u32[]{:S(2)}) collective-permute-start(bf16[64,256]{1,0:T(8,128)(2,1)S(1)} %fusion.45), channel_id=1, source_target_pairs={{0,48},{4,52},{8,56},{12,60},{16,64},{20,68},{24,72},{28,76},{32,8... | collective-permute-start | bytes 98312 | tf_op jit(solution)/shard_map/ppermute | solution.py:11
  101.2 11.5 %collective-permute-start.19 = (bf16[64,256]{1,0:T(8,128)(2,1)S(1)}, bf16[64,256]{1,0:T(8,128)(2,1)S(1)}, u32[]{:S(2)}, u32[]{:S(2)}) collective-permute-start(bf16[64,256]{1,0:T(8,128)(2,1)S(1)} %fusion.45), channel_id=1, source_target_pairs={{48,0},{52,4},{56,8},{60,12},{64,16},{68,20},{72,24},{76,28},{80,3... | collective-permute-start | bytes 98312 | tf_op jit(solution)/shard_map/ppermute | solution.py:11
  112.7 7.4 %collective-permute-start.18 = (bf16[64,256]{1,0:T(8,128)(2,1)S(1)}, bf16[64,256]{1,0:T(8,128)(2,1)S(1)}, u32[]{:S(2)}, u32[]{:S(2)}) collective-permute-start(bf16[64,256]{1,0:T(8,128)(2,1)S(1)} %fusion.45), channel_id=1, source_target_pairs={{0,32},{4,36},{8,40},{12,44},{16,48},{20,52},{24,56},{28,60},{32,6... | collective-permute-start | bytes 98312 | tf_op jit(solution)/shard_map/ppermute | solution.py:11
  120.0 122.4 %collective-permute-start.17 = (bf16[64,256]{1,0:T(8,128)(2,1)S(1)}, bf16[64,256]{1,0:T(8,128)(2,1)}, u32[]{:S(2)}, u32[]{:S(2)}) collective-permute-start(bf16[64,256]{1,0:T(8,128)(2,1)S(1)} %fusion.45), channel_id=1, source_target_pairs={{32,0},{36,4},{40,8},{44,12},{48,16},{52,20},{56,24},{60,28},{64,3... | collective-permute-start | bytes 98312 | tf_op jit(solution)/shard_map/ppermute | solution.py:11
  121.7 19.9 %collective-permute-start.16 = (bf16[64,256]{1,0:T(8,128)(2,1)S(1)}, bf16[64,256]{1,0:T(8,128)(2,1)S(1)}, u32[]{:S(2)}, u32[]{:S(2)}) collective-permute-start(bf16[64,256]{1,0:T(8,128)(2,1)S(1)} %fusion.46), channel_id=1, source_target_pairs={{0,96},{4,100},{8,104},{12,108},{16,112},{20,116},{24,120},{28,124... | collective-permute-start | bytes 98312 | tf_op jit(solution)/shard_map/ppermute | solution.py:11
  132.5 7.5 %collective-permute-start.3 = (bf16[64,256]{1,0:T(8,128)(2,1)S(1)}, bf16[64,256]{1,0:T(8,128)(2,1)S(1)}, u32[]{:S(2)}, u32[]{:S(2)}) collective-permute-start(bf16[64,256]{1,0:T(8,128)(2,1)S(1)} %fusion.46), channel_id=1, source_target_pairs={{0,32},{32,0},{4,36},{36,4},{8,40},{40,8},{12,44},{44,12},{16,48},... | collective-permute-start | bytes 98312 | tf_op jit(solution)/shard_map/ppermute | solution.py:41
  140.0 7.6 %collective-permute-start.15 = (bf16[64,256]{1,0:T(8,128)(2,1)S(1)}, bf16[64,256]{1,0:T(8,128)(2,1)S(1)}, u32[]{:S(2)}, u32[]{:S(2)}) collective-permute-start(bf16[64,256]{1,0:T(8,128)(2,1)S(1)} %fusion.46), channel_id=1, source_target_pairs={{96,0},{100,4},{104,8},{108,12},{112,16},{116,20},{120,24},{124,28... | collective-permute-start | bytes 98312 | tf_op jit(solution)/shard_map/ppermute | solution.py:11
  141.6 7.5 %collective-permute-start.14 = (bf16[64,256]{1,0:T(8,128)(2,1)S(1)}, bf16[64,256]{1,0:T(8,128)(2,1)S(1)}, u32[]{:S(2)}, u32[]{:S(2)}) collective-permute-start(bf16[64,256]{1,0:T(8,128)(2,1)S(1)} %fusion.46), channel_id=1, source_target_pairs={{0,64},{4,68},{8,72},{12,76},{16,80},{20,84},{24,88},{28,92},{32,9... | collective-permute-start | bytes 98312 | tf_op jit(solution)/shard_map/ppermute | solution.py:11
  147.6 93.8 %collective-permute-start.13 = (bf16[64,256]{1,0:T(8,128)(2,1)S(1)}, bf16[64,256]{1,0:T(8,128)(2,1)}, u32[]{:S(2)}, u32[]{:S(2)}) collective-permute-start(bf16[64,256]{1,0:T(8,128)(2,1)S(1)} %fusion.46), channel_id=1, source_target_pairs={{64,0},{68,4},{72,8},{76,12},{80,16},{84,20},{88,24},{92,28},{96,3... | collective-permute-start | bytes 98312 | tf_op jit(solution)/shard_map/ppermute | solution.py:11
  149.0 10.0 %collective-permute-start.4 = (bf16[64,256]{1,0:T(8,128)(2,1)S(1)}, bf16[64,256]{1,0:T(8,128)(2,1)S(1)}, u32[]{:S(2)}, u32[]{:S(2)}) collective-permute-start(bf16[64,256]{1,0:T(8,128)(2,1)S(1)} %fusion.47), channel_id=1, source_target_pairs={{0,64},{64,0},{4,68},{68,4},{8,72},{72,8},{12,76},{76,12},{16,80},... | collective-permute-start | bytes 98312 | tf_op jit(solution)/shard_map/ppermute | solution.py:41
  159.0 12.1 %collective-permute-start.12 = (bf16[64,256]{1,0:T(8,128)(2,1)S(1)}, bf16[64,256]{1,0:T(8,128)(2,1)S(1)}, u32[]{:S(2)}, u32[]{:S(2)}) collective-permute-start(bf16[64,256]{1,0:T(8,128)(2,1)S(1)} %fusion.47), channel_id=1, source_target_pairs={{0,192},{4,196},{8,200},{12,204},{16,208},{20,212},{24,216},{28,22... | collective-permute-start | bytes 98312 | tf_op jit(solution)/shard_map/ppermute | solution.py:11
  171.1 11.8 %collective-permute-start.11 = (bf16[64,256]{1,0:T(8,128)(2,1)S(1)}, bf16[64,256]{1,0:T(8,128)(2,1)S(1)}, u32[]{:S(2)}, u32[]{:S(2)}) collective-permute-start(bf16[64,256]{1,0:T(8,128)(2,1)S(1)} %fusion.47), channel_id=1, source_target_pairs={{192,0},{196,4},{200,8},{204,12},{208,16},{212,20},{216,24},{220,2... | collective-permute-start | bytes 98312 | tf_op jit(solution)/shard_map/ppermute | solution.py:11
  182.9 6.8 %collective-permute-start.10 = (bf16[64,256]{1,0:T(8,128)(2,1)S(1)}, bf16[64,256]{1,0:T(8,128)(2,1)S(1)}, u32[]{:S(2)}, u32[]{:S(2)}) collective-permute-start(bf16[64,256]{1,0:T(8,128)(2,1)S(1)} %fusion.47), channel_id=1, source_target_pairs={{0,128},{4,132},{8,136},{12,140},{16,144},{20,148},{24,152},{28,15... | collective-permute-start | bytes 98312 | tf_op jit(solution)/shard_map/ppermute | solution.py:11
  189.7 13.5 %collective-permute-start.8 = (bf16[64,256]{1,0:T(8,128)(2,1)S(1)}, bf16[64,256]{1,0:T(8,128)(2,1)S(1)}, u32[]{:S(2)}, u32[]{:S(2)}) collective-permute-start(bf16[64,256]{1,0:T(8,128)(2,1)S(1)} %fusion.48), channel_id=1, source_target_pairs={{0,384},{4,388},{8,392},{12,396},{16,400},{20,404},{24,408},{28,41... | collective-permute-start | bytes 98312 | tf_op jit(solution)/shard_map/ppermute | solution.py:11
  203.3 9.7 %collective-permute-start.7 = (bf16[64,256]{1,0:T(8,128)(2,1)S(1)}, bf16[64,256]{1,0:T(8,128)(2,1)S(1)}, u32[]{:S(2)}, u32[]{:S(2)}) collective-permute-start(bf16[64,256]{1,0:T(8,128)(2,1)S(1)} %fusion.48), channel_id=1, source_target_pairs={{384,0},{388,4},{392,8},{396,12},{400,16},{404,20},{408,24},{412,2... | collective-permute-start | bytes 98312 | tf_op jit(solution)/shard_map/ppermute | solution.py:11
  213.0 2.9 %collective-permute-start.6 = (bf16[64,256]{1,0:T(8,128)(2,1)S(1)}, bf16[64,256]{1,0:T(8,128)(2,1)S(1)}, u32[]{:S(2)}, u32[]{:S(2)}) collective-permute-start(bf16[64,256]{1,0:T(8,128)(2,1)S(1)} %fusion.48), channel_id=1, source_target_pairs={{0,256},{4,260},{8,264},{12,268},{16,272},{20,276},{24,280},{28,28... | collective-permute-start | bytes 98312 | tf_op jit(solution)/shard_map/ppermute | solution.py:11
  215.9 14.5 %collective-permute-start.5 = (bf16[64,256]{1,0:T(8,128)(2,1)S(1)}, bf16[64,256]{1,0:T(8,128)(2,1)S(1)}, u32[]{:S(2)}, u32[]{:S(2)}) collective-permute-start(bf16[64,256]{1,0:T(8,128)(2,1)S(1)} %fusion.48), channel_id=1, source_target_pairs={{256,0},{260,4},{264,8},{268,12},{272,16},{276,20},{280,24},{284,2... | collective-permute-start | bytes 98312 | tf_op jit(solution)/shard_map/ppermute | solution.py:11
  230.4 1.3 copy-start.5
  230.4 10.0 %collective-permute-start.9 = (bf16[64,256]{1,0:T(8,128)(2,1)S(1)}, bf16[64,256]{1,0:T(8,128)(2,1)}, u32[]{:S(2)}, u32[]{:S(2)}) collective-permute-start(bf16[64,256]{1,0:T(8,128)(2,1)S(1)} %fusion.47), channel_id=1, source_target_pairs={{128,0},{132,4},{136,8},{140,12},{144,16},{148,20},{152,24},{156,2... | collective-permute-start | bytes 98312 | tf_op jit(solution)/shard_map/ppermute | solution.py:11
  259.6 2.7 copy-start.3
Sparse Core Ops, SparseCore 0:
  140.1 44.6 all-gather.2
where the time goes:
time: 278 us; the launch traced here: 277 us
  starting transfers between devices  118 us (42%)
  waiting for transfers between devices  69.9 us (25%)
  between operations  31.4 us (11%)
  blocking collectives  27.6 us (10%)
  matrix products  18.7 us (7%)
  local copies, waits for them, and re-layouts  5.31 us (2%)
  other arithmetic  4.5 us (2%)
    ppermute x24, starting transfers between devices, shifted(): lax.ppermute(value, axis, [(source, source + steps) for source in range(l...  90.3 us
    ppermute x24, waiting for transfers between devices, shifted(): lax.ppermute(value, axis, [(source, source + steps) for source in range(l...  62.3 us
    ppermute x5, starting transfers between devices, swapped(): return lax.ppermute(block, axis, route)  24.2 us
    all_gather x1, blocking collectives, per_device(): lax.all_gather(leaf_coef[None], 'level', axis=0, tiled=True)  15.7 us
    all_gather x1, blocking collectives, per_device(): fields = lax.all_gather(fields, 'level', axis=0, tiled=True)  12 us
    dot_general x19, matrix products, down_one(): lax.dot_general(fields, matrix, (((1,), (1,)), ((), ())), preferred_eleme...  7.76 us
    ppermute x5, waiting for transfers between devices, swapped(): return lax.ppermute(block, axis, route)  7.52 us
  transfers between devices with their start and end apart: 32, of which 16 were waited for; matrix products, arithmetic and copies ran while one was open for 6% of the time, Pallas kernels for 0%

commit v1 on v0

--- a/solution.py
+++ b/solution.py
@@ -3,6 +3,13 @@
 import jax.numpy as jnp
 from jax import lax
 from jax.sharding import PartitionSpec as P
+
+
+def swapped_in(block, name, dim):
+    count = lax.axis_size(name)
+    blocks = jnp.stack([block for _ in range(count)])
+    blocks = lax.all_to_all(blocks, name, split_axis=0, concat_axis=0)
+    return jnp.concatenate(blocks, axis=dim)
 
 
 def shifted(value, axis, steps):
@@ -83,7 +90,7 @@
     padded = with_halo(points_x, (("leaf", 1),), points)
     left_g, own_g, right_g, group_coef = (
         *in_one_piece((padded[:, :points], points_x, padded[:, 2 * points :]), "level", 1, 0),
-        lax.all_gather(leaf_coef[None], "level", axis=0, tiled=True),
+        swapped_in(leaf_coef[None], "level", 0),
     )
     window_x = jnp.concatenate([left_g, own_g, right_g], axis=1)
     level_coefs = [group_coef[member] for member in range(group_size)]

time: 278 us -> 261 us (0.939)
  blocking collectives: 27.6 us -> 12 us
  waiting for transfers between devices: 69.9 us -> 55.9 us
  starting transfers between devices: 118 us -> 131 us
    all_gather x1 -> x0, blocking collectives: 15.7 us -> none  [per_device(): lax.all_gather(leaf_coef[None], 'level', axis=0, tiled=True)]
    ppermute x24, waiting for transfers between devices: 62.3 us -> 48.9 us  [shifted(): lax.ppermute(value, axis, [(source, source + steps) for source in range(l...]
    all_to_all x0 -> x1, starting transfers between devices: none -> 9.32 us  [swapped_in(): blocks = lax.all_to_all(blocks, name, split_axis=0, concat_axis=0)]
    ppermute x5, starting transfers between devices: 24.2 us -> 29.1 us  [swapped(): return lax.ppermute(block, axis, route)]
  transfers between devices with their start and end apart: 32 -> 33, of which waited for: 16 -> 13; matrix products, arithmetic and copies ran while one was open for 6% -> 5% of each run, Pallas kernels for 0% -> 0%
where the time goes in v1:
time: 261 us; the launch traced here: 260 us
  starting transfers between devices  131 us (50%)
  waiting for transfers between devices  55.9 us (21%)
  between operations  31.8 us (12%)
  matrix products  17.7 us (7%)
  blocking collectives  12 us (5%)
  local copies, waits for them, and re-layouts  7.03 us (3%)
  other arithmetic  3.48 us (1%)
    ppermute x24, starting transfers between devices, shifted(): lax.ppermute(value, axis, [(source, source + steps) for source in range(l...  90 us
    ppermute x24, waiting for transfers between devices, shifted(): lax.ppermute(value, axis, [(source, source + steps) for source in range(l...  48.9 us
    ppermute x5, starting transfers between devices, swapped(): return lax.ppermute(block, axis, route)  29.1 us
    all_gather x1, blocking collectives, per_device(): fields = lax.all_gather(fields, 'level', axis=0, tiled=True)  12 us
    all_to_all x1, starting transfers between devices, swapped_in(): blocks = lax.all_to_all(blocks, name, split_axis=0, concat_axis=0)  9.32 us
    dot_general x19, matrix products, down_one(): lax.dot_general(fields, matrix, (((1,), (1,)), ((), ())), preferred_eleme...  7.76 us
    ppermute x5, waiting for transfers between devices, swapped(): return lax.ppermute(block, axis, route)  6.88 us
    dot_general x4, matrix products, add_tile(): jnp.dot(column_x, tile_block, preferred_element_type=jnp.float32)  5.27 us
  transfers between devices with their start and end apart: 33, of which 13 were waited for; matrix products, arithmetic and copies ran while one was open for 5% of the time, Pallas kernels for 0%

profile of v1, /device:TPU:2, one launch (start us, length us, event | category | flops | bytes accessed | tf_op | source)
XLA Modules:
  0.0 259.6 jit_solution(4513044661727682104)
XLA Ops:
  6.5 0.9 copy-done
  7.5 1.2 convolution_convert_fusion
  9.5 9.3 %all-to-all-start = ((bf16[4,1,256,256]{3,2,1,0:T(8,128)(2,1)}), bf16[4,1,256,256]{3,2,1,0:T(8,128)(2,1)S(1)}, u32[]{:S(2)}, u32[]{:S(2)}) async-start(bf16[4,1,256,256]{3,2,1,0:T(8,128)(2,1)} %stack.3), calls=%async_computation | async-start | bytes 1048576 | tf_op jit(solution)/shard_map/all_to_all | solution.py:11
  18.8 1.3 collective-permute-start.29
  20.1 1.3 collective-permute-start.30
  41.8 3.2 %collective-permute-start = (bf16[64,256]{1,0:T(8,128)(2,1)S(1)}, bf16[64,256]{1,0:T(8,128)(2,1)S(1)}, u32[]{:S(2)}, u32[]{:S(2)}) collective-permute-start(bf16[64,256]{1,0:T(8,128)(2,1)S(1)} %fusion.160), channel_id=1, source_target_pairs={{0,4},{4,0},{8,12},{12,8},{16,20},{20,16},{24,28},{28,24},{32,36},... | collective-permute-start | bytes 98312 | tf_op jit(solution)/shard_map/ppermute | solution.py:48
  45.0 0.9 pad_maximum_fusion.1
  46.0 1.3 collective-permute-start.27
  47.3 1.3 collective-permute-start.26
  48.6 1.3 collective-permute-start.25
  49.9 7.0 %collective-permute-start.28 = (bf16[64,256]{1,0:T(8,128)(2,1)S(1)}, bf16[64,256]{1,0:T(8,128)(2,1)S(1)}, u32[]{:S(2)}, u32[]{:S(2)}) collective-permute-start(bf16[64,256]{1,0:T(8,128)(2,1)S(1)} %fusion.160), channel_id=1, source_target_pairs={{0,12},{4,16},{8,20},{12,24},{16,28},{20,32},{24,36},{28,40},{32,4... | collective-permute-start | bytes 98312 | tf_op jit(solution)/shard_map/ppermute | solution.py:18
  57.2 6.5 %collective-permute-start.24 = (bf16[64,256]{1,0:T(8,128)(2,1)S(1)}, bf16[64,256]{1,0:T(8,128)(2,1)S(1)}, u32[]{:S(2)}, u32[]{:S(2)}) collective-permute-start(bf16[64,256]{1,0:T(8,128)(2,1)S(1)} %fusion.44), channel_id=1, source_target_pairs={{0,24},{4,28},{8,32},{12,36},{16,40},{20,44},{24,48},{28,52},{32,5... | collective-permute-start | bytes 98312 | tf_op jit(solution)/shard_map/ppermute | solution.py:18
  63.7 1.3 collective-permute-start.23
  65.2 1.3 collective-permute-start.22
  66.7 7.2 %collective-permute-start.1 = (bf16[64,256]{1,0:T(8,128)(2,1)S(1)}, bf16[64,256]{1,0:T(8,128)(2,1)S(1)}, u32[]{:S(2)}, u32[]{:S(2)}) collective-permute-start(bf16[64,256]{1,0:T(8,128)(2,1)S(1)} %fusion.44), channel_id=1, source_target_pairs={{0,8},{8,0},{4,12},{12,4},{16,24},{24,16},{20,28},{28,20},{32,40},... | collective-permute-start | bytes 98312 | tf_op jit(solution)/shard_map/ppermute | solution.py:48
  74.1 1.7 collective-permute-done.1
  75.8 1.3 collective-permute-start.21
  77.4 7.4 %collective-permute-start.20 = (bf16[64,256]{1,0:T(8,128)(2,1)S(1)}, bf16[64,256]{1,0:T(8,128)(2,1)S(1)}, u32[]{:S(2)}, u32[]{:S(2)}) collective-permute-start(bf16[64,256]{1,0:T(8,128)(2,1)S(1)} %fusion.45), channel_id=1, source_target_pairs={{0,48},{4,52},{8,56},{12,60},{16,64},{20,68},{24,72},{28,76},{32,8... | collective-permute-start | bytes 98312 | tf_op jit(solution)/shard_map/ppermute | solution.py:18
  85.0 1.3 collective-permute-start.19
  86.5 5.6 %collective-permute-start.2 = (bf16[64,256]{1,0:T(8,128)(2,1)S(1)}, bf16[64,256]{1,0:T(8,128)(2,1)S(1)}, u32[]{:S(2)}, u32[]{:S(2)}) collective-permute-start(bf16[64,256]{1,0:T(8,128)(2,1)S(1)} %fusion.45), channel_id=1, source_target_pairs={{0,16},{16,0},{4,20},{20,4},{8,24},{24,8},{12,28},{28,12},{32,48},... | collective-permute-start | bytes 98312 | tf_op jit(solution)/shard_map/ppermute | solution.py:48
  92.3 1.7 collective-permute-done.2
  94.0 8.0 %collective-permute-start.18 = (bf16[64,256]{1,0:T(8,128)(2,1)S(1)}, bf16[64,256]{1,0:T(8,128)(2,1)S(1)}, u32[]{:S(2)}, u32[]{:S(2)}) collective-permute-start(bf16[64,256]{1,0:T(8,128)(2,1)S(1)} %fusion.45), channel_id=1, source_target_pairs={{0,32},{4,36},{8,40},{12,44},{16,48},{20,52},{24,56},{28,60},{32,6... | collective-permute-start | bytes 98312 | tf_op jit(solution)/shard_map/ppermute | solution.py:18
  102.3 1.3 collective-permute-start.17
  103.8 12.2 %collective-permute-start.16 = (bf16[64,256]{1,0:T(8,128)(2,1)S(1)}, bf16[64,256]{1,0:T(8,128)(2,1)S(1)}, u32[]{:S(2)}, u32[]{:S(2)}) collective-permute-start(bf16[64,256]{1,0:T(8,128)(2,1)S(1)} %fusion.46), channel_id=1, source_target_pairs={{0,96},{4,100},{8,104},{12,108},{16,112},{20,116},{24,120},{28,124... | collective-permute-start | bytes 98312 | tf_op jit(solution)/shard_map/ppermute | solution.py:18
  116.2 5.1 %collective-permute-start.3 = (bf16[64,256]{1,0:T(8,128)(2,1)S(1)}, bf16[64,256]{1,0:T(8,128)(2,1)S(1)}, u32[]{:S(2)}, u32[]{:S(2)}) collective-permute-start(bf16[64,256]{1,0:T(8,128)(2,1)S(1)} %fusion.46), channel_id=1, source_target_pairs={{0,32},{32,0},{4,36},{36,4},{8,40},{40,8},{12,44},{44,12},{16,48},... | collective-permute-start | bytes 98312 | tf_op jit(solution)/shard_map/ppermute | solution.py:48
  121.5 1.7 collective-permute-done.3
  123.2 1.3 collective-permute-start.15
  124.8 2.7 %collective-permute-start.14 = (bf16[64,256]{1,0:T(8,128)(2,1)S(1)}, bf16[64,256]{1,0:T(8,128)(2,1)S(1)}, u32[]{:S(2)}, u32[]{:S(2)}) collective-permute-start(bf16[64,256]{1,0:T(8,128)(2,1)S(1)} %fusion.46), channel_id=1, source_target_pairs={{0,64},{4,68},{8,72},{12,76},{16,80},{20,84},{24,88},{28,92},{32,9... | collective-permute-start | bytes 98312 | tf_op jit(solution)/shard_map/ppermute | solution.py:18
  127.6 3.2 %collective-permute-done.15 = bf16[64,256]{1,0:T(8,128)(2,1)S(1)} collective-permute-done((bf16[64,256]{1,0:T(8,128)(2,1)S(1)}, bf16[64,256]{1,0:T(8,128)(2,1)S(1)}, u32[]{:S(2)}, u32[]{:S(2)}) %collective-permute-start.15) | collective-permute-done | bytes 32800 | tf_op jit(solution)/shard_map/ppermute | solution.py:18
  130.8 1.3 collective-permute-start.13
  132.2 7.9 %collective-permute-start.4 = (bf16[64,256]{1,0:T(8,128)(2,1)S(1)}, bf16[64,256]{1,0:T(8,128)(2,1)S(1)}, u32[]{:S(2)}, u32[]{:S(2)}) collective-permute-start(bf16[64,256]{1,0:T(8,128)(2,1)S(1)} %fusion.47), channel_id=1, source_target_pairs={{0,64},{64,0},{4,68},{68,4},{8,72},{72,8},{12,76},{76,12},{16,80},... | collective-permute-start | bytes 98312 | tf_op jit(solution)/shard_map/ppermute | solution.py:48
  140.3 1.7 collective-permute-done.4
  142.1 9.8 %collective-permute-start.12 = (bf16[64,256]{1,0:T(8,128)(2,1)S(1)}, bf16[64,256]{1,0:T(8,128)(2,1)S(1)}, u32[]{:S(2)}, u32[]{:S(2)}) collective-permute-start(bf16[64,256]{1,0:T(8,128)(2,1)S(1)} %fusion.47), channel_id=1, source_target_pairs={{0,192},{4,196},{8,200},{12,204},{16,208},{20,212},{24,216},{28,22... | collective-permute-start | bytes 98312 | tf_op jit(solution)/shard_map/ppermute | solution.py:18
  152.2 1.3 collective-permute-done.12
  153.5 1.3 collective-permute-start.11
  154.9 10.4 %collective-permute-done.11 = bf16[64,256]{1,0:T(8,128)(2,1)S(1)} collective-permute-done((bf16[64,256]{1,0:T(8,128)(2,1)S(1)}, bf16[64,256]{1,0:T(8,128)(2,1)S(1)}, u32[]{:S(2)}, u32[]{:S(2)}) %collective-permute-start.11) | collective-permute-done | bytes 32800 | tf_op jit(solution)/shard_map/ppermute | solution.py:18
  165.3 6.3 %collective-permute-start.10 = (bf16[64,256]{1,0:T(8,128)(2,1)S(1)}, bf16[64,256]{1,0:T(8,128)(2,1)S(1)}, u32[]{:S(2)}, u32[]{:S(2)}) collective-permute-start(bf16[64,256]{1,0:T(8,128)(2,1)S(1)} %fusion.47), channel_id=1, source_target_pairs={{0,128},{4,132},{8,136},{12,140},{16,144},{20,148},{24,152},{28,15... | collective-permute-start | bytes 98312 | tf_op jit(solution)/shard_map/ppermute | solution.py:18
  171.7 1.4 collective-permute-done.10
  173.2 10.9 %collective-permute-start.8 = (bf16[64,256]{1,0:T(8,128)(2,1)S(1)}, bf16[64,256]{1,0:T(8,128)(2,1)S(1)}, u32[]{:S(2)}, u32[]{:S(2)}) collective-permute-start(bf16[64,256]{1,0:T(8,128)(2,1)S(1)} %fusion.48), channel_id=1, source_target_pairs={{0,384},{4,388},{8,392},{12,396},{16,400},{20,404},{24,408},{28,41... | collective-permute-start | bytes 98312 | tf_op jit(solution)/shard_map/ppermute | solution.py:18
  184.2 2.3 collective-permute-done.8
  186.5 1.3 collective-permute-start.7
  187.9 8.3 %collective-permute-done.7 = bf16[64,256]{1,0:T(8,128)(2,1)S(1)} collective-permute-done((bf16[64,256]{1,0:T(8,128)(2,1)S(1)}, bf16[64,256]{1,0:T(8,128)(2,1)S(1)}, u32[]{:S(2)}, u32[]{:S(2)}) %collective-permute-start.7) | collective-permute-done | bytes 32800 | tf_op jit(solution)/shard_map/ppermute | solution.py:18
  196.2 1.3 collective-permute-start.6
  197.6 1.4 collective-permute-done.6
  199.0 1.3 collective-permute-start.5
  200.5 13.1 %collective-permute-done.5 = bf16[64,256]{1,0:T(8,128)(2,1)S(1)} collective-permute-done((bf16[64,256]{1,0:T(8,128)(2,1)S(1)}, bf16[64,256]{1,0:T(8,128)(2,1)S(1)}, u32[]{:S(2)}, u32[]{:S(2)}) %collective-permute-start.5) | collective-permute-done | bytes 32800 | tf_op jit(solution)/shard_map/ppermute | solution.py:18
  213.5 1.3 collective-permute-start.9
  214.8 1.0 fusion.55
  215.9 7.5 %collective-permute-done.9 = bf16[64,256]{1,0:T(8,128)(2,1)} collective-permute-done((bf16[64,256]{1,0:T(8,128)(2,1)S(1)}, bf16[64,256]{1,0:T(8,128)(2,1)}, u32[]{:S(2)}, u32[]{:S(2)}) %collective-permute-start.9) | collective-permute-done | bytes 32800 | tf_op jit(solution)/shard_map/ppermute | solution.py:18
  223.4 1.0 fusion.56
  224.4 1.0 fusion.57
  225.5 1.0 fusion.58
  226.5 1.0 fusion.59
  227.8 12.0 %all_gather.6 = bf16[256,256]{1,0:T(8,128)(2,1)S(1)} all-gather(bf16[64,256]{1,0:T(8,128)(2,1)S(1)} %fusion.49), channel_id=1, replica_groups=mesh['leaf'=128,'level'=4] {'level'}, dimensions={0}, use_global_device_ids=true | all-gather | bytes 163840 | tf_op jit(solution)/shard_map/all_gather | solution.py:139
  240.4 2.2 fusion.211
  242.7 1.8 pad_maximum_fusion
  245.4 1.3 conditional.7
  245.4 1.3 convolution_add_fusion.1
  246.8 1.4 conditional.8
  246.8 1.3 convolution_add_fusion.2
  248.1 1.4 conditional.9
  248.1 1.3 convolution_add_fusion.3
  249.5 2.5 conditional.11
  250.7 1.3 convolution_add_fusion
  (78 shorter events, 10.9 us)
Async XLA Ops:
  6.5 1.0 copy-start
  6.5 12.3 %copy-start.4 = (bf16[256,512]{1,0:T(8,128)(2,1)S(1)}, bf16[256,512]{1,0:T(8,128)(2,1)}, u32[]{:S(2)}) copy-start(bf16[256,512]{1,0:T(8,128)(2,1)} %param.16) | copy-start | bytes 786436
  6.5 15.6 %copy-start.7 = (s32[1,4]{1,0:T(1,128)S(1)}, s32[1,4]{1,0:T(1,128)}, u32[]{:S(2)}) copy-start(s32[1,4]{1,0:T(1,128)} %param.19) | copy-start | bytes 52
  6.5 18.2 %copy-start.6 = (s32[6,128,2]{1,2,0:T(2,128)S(1)}, s32[6,128,2]{1,2,0:T(2,128)}, u32[]{:S(2)}) copy-start(s32[6,128,2]{1,2,0:T(2,128)} %param.23) | copy-start | bytes 18436
  6.5 34.2 %copy-start.1 = (bf16[2,256,256]{2,1,0:T(8,128)(2,1)S(1)}, bf16[2,256,256]{2,1,0:T(8,128)(2,1)}, u32[]{:S(2)}) copy-start(bf16[2,256,256]{2,1,0:T(8,128)(2,1)} %param.21) | copy-start | bytes 786436
  9.5 31.2 %all-to-all-start = ((bf16[4,1,256,256]{3,2,1,0:T(8,128)(2,1)}), bf16[4,1,256,256]{3,2,1,0:T(8,128)(2,1)S(1)}, u32[]{:S(2)}, u32[]{:S(2)}) async-start(bf16[4,1,256,256]{3,2,1,0:T(8,128)(2,1)} %stack.3), calls=%async_computation | async-start | bytes 1048576 | tf_op jit(solution)/shard_map/all_to_all | solution.py:11
  18.8 221.6 %all-gather.2.cloned.1.call-start = ((), (), s32[]{:S(2)}) async-start(), calls=%async_computation.1 | async-start | bytes 3932160 | tf_op jit(solution)/shard_map/all_gather | solution.py:37
  18.8 26.2 %collective-permute-start.29 = (bf16[256,512]{1,0:T(8,128)(2,1)S(1)}, bf16[256,512]{1,0:T(8,128)(2,1)S(1)}, u32[]{:S(2)}, u32[]{:S(2)}) collective-permute-start(bf16[256,512]{1,0:T(8,128)(2,1)S(1)} %copy-done.4), channel_id=1, source_target_pairs={{0,4},{4,8},{8,12},{12,16},{16,20},{20,24},{24,28},{28,32},{32,36}... | collective-permute-start | bytes 786440 | tf_op jit(solution)/shard_map/ppermute | solution.py:26
  20.1 24.9 %collective-permute-start.30 = (bf16[256,512]{1,0:T(8,128)(2,1)S(1)}, bf16[256,512]{1,0:T(8,128)(2,1)S(1)}, u32[]{:S(2)}, u32[]{:S(2)}) collective-permute-start(bf16[256,512]{1,0:T(8,128)(2,1)S(1)} %copy-done.4), channel_id=1, source_target_pairs={{4,0},{8,4},{12,8},{16,12},{20,16},{24,20},{28,24},{32,28},{36,32}... | collective-permute-start | bytes 786440 | tf_op jit(solution)/shard_map/ppermute | solution.py:29
  41.8 23.2 %copy-start.2 = (bf16[6,2,256,256]{3,2,1,0:T(8,128)(2,1)S(1)}, bf16[6,2,256,256]{3,2,1,0:T(8,128)(2,1)}, u32[]{:S(2)}) copy-start(bf16[6,2,256,256]{3,2,1,0:T(8,128)(2,1)} %param.22) | copy-start | bytes 4718596
  41.8 15.0 %collective-permute-start = (bf16[64,256]{1,0:T(8,128)(2,1)S(1)}, bf16[64,256]{1,0:T(8,128)(2,1)S(1)}, u32[]{:S(2)}, u32[]{:S(2)}) collective-permute-start(bf16[64,256]{1,0:T(8,128)(2,1)S(1)} %fusion.160), channel_id=1, source_target_pairs={{0,4},{4,0},{8,12},{12,8},{16,20},{20,16},{24,28},{28,24},{32,36},... | collective-permute-start | bytes 98312 | tf_op jit(solution)/shard_map/ppermute | solution.py:48
  46.0 17.7 %collective-permute-start.27 = (bf16[64,256]{1,0:T(8,128)(2,1)S(1)}, bf16[64,256]{1,0:T(8,128)(2,1)S(1)}, u32[]{:S(2)}, u32[]{:S(2)}) collective-permute-start(bf16[64,256]{1,0:T(8,128)(2,1)S(1)} %fusion.160), channel_id=1, source_target_pairs={{12,0},{16,4},{20,8},{24,12},{28,16},{32,20},{36,24},{40,28},{44,3... | collective-permute-start | bytes 98312 | tf_op jit(solution)/shard_map/ppermute | solution.py:18
  47.3 17.9 %collective-permute-start.26 = (bf16[64,256]{1,0:T(8,128)(2,1)S(1)}, bf16[64,256]{1,0:T(8,128)(2,1)S(1)}, u32[]{:S(2)}, u32[]{:S(2)}) collective-permute-start(bf16[64,256]{1,0:T(8,128)(2,1)S(1)} %fusion.160), channel_id=1, source_target_pairs={{0,8},{4,12},{8,16},{12,20},{16,24},{20,28},{24,32},{28,36},{32,40... | collective-permute-start | bytes 98312 | tf_op jit(solution)/shard_map/ppermute | solution.py:18
  48.6 179.0 %collective-permute-start.25 = (bf16[64,256]{1,0:T(8,128)(2,1)S(1)}, bf16[64,256]{1,0:T(8,128)(2,1)S(1)}, u32[]{:S(2)}, u32[]{:S(2)}) collective-permute-start(bf16[64,256]{1,0:T(8,128)(2,1)S(1)} %fusion.160), channel_id=1, source_target_pairs={{8,0},{12,4},{16,8},{20,12},{24,16},{28,20},{32,24},{36,28},{40,32... | collective-permute-start | bytes 98312 | tf_op jit(solution)/shard_map/ppermute | solution.py:18
  49.9 16.8 %collective-permute-start.28 = (bf16[64,256]{1,0:T(8,128)(2,1)S(1)}, bf16[64,256]{1,0:T(8,128)(2,1)S(1)}, u32[]{:S(2)}, u32[]{:S(2)}) collective-permute-start(bf16[64,256]{1,0:T(8,128)(2,1)S(1)} %fusion.160), channel_id=1, source_target_pairs={{0,12},{4,16},{8,20},{12,24},{16,28},{20,32},{24,36},{28,40},{32,4... | collective-permute-start | bytes 98312 | tf_op jit(solution)/shard_map/ppermute | solution.py:18
  57.2 20.2 %collective-permute-start.24 = (bf16[64,256]{1,0:T(8,128)(2,1)S(1)}, bf16[64,256]{1,0:T(8,128)(2,1)S(1)}, u32[]{:S(2)}, u32[]{:S(2)}) collective-permute-start(bf16[64,256]{1,0:T(8,128)(2,1)S(1)} %fusion.44), channel_id=1, source_target_pairs={{0,24},{4,28},{8,32},{12,36},{16,40},{20,44},{24,48},{28,52},{32,5... | collective-permute-start | bytes 98312 | tf_op jit(solution)/shard_map/ppermute | solution.py:18
  63.7 21.3 %collective-permute-start.23 = (bf16[64,256]{1,0:T(8,128)(2,1)S(1)}, bf16[64,256]{1,0:T(8,128)(2,1)S(1)}, u32[]{:S(2)}, u32[]{:S(2)}) collective-permute-start(bf16[64,256]{1,0:T(8,128)(2,1)S(1)} %fusion.44), channel_id=1, source_target_pairs={{24,0},{28,4},{32,8},{36,12},{40,16},{44,20},{48,24},{52,28},{56,3... | collective-permute-start | bytes 98312 | tf_op jit(solution)/shard_map/ppermute | solution.py:18
  65.2 21.3 %collective-permute-start.22 = (bf16[64,256]{1,0:T(8,128)(2,1)S(1)}, bf16[64,256]{1,0:T(8,128)(2,1)S(1)}, u32[]{:S(2)}, u32[]{:S(2)}) collective-permute-start(bf16[64,256]{1,0:T(8,128)(2,1)S(1)} %fusion.44), channel_id=1, source_target_pairs={{0,16},{4,20},{8,24},{12,28},{16,32},{20,36},{24,40},{28,44},{32,4... | collective-permute-start | bytes 98312 | tf_op jit(solution)/shard_map/ppermute | solution.py:18
  66.7 9.1 %collective-permute-start.1 = (bf16[64,256]{1,0:T(8,128)(2,1)S(1)}, bf16[64,256]{1,0:T(8,128)(2,1)S(1)}, u32[]{:S(2)}, u32[]{:S(2)}) collective-permute-start(bf16[64,256]{1,0:T(8,128)(2,1)S(1)} %fusion.44), channel_id=1, source_target_pairs={{0,8},{8,0},{4,12},{12,4},{16,24},{24,16},{20,28},{28,20},{32,40},... | collective-permute-start | bytes 98312 | tf_op jit(solution)/shard_map/ppermute | solution.py:48
  75.8 150.7 %collective-permute-start.21 = (bf16[64,256]{1,0:T(8,128)(2,1)S(1)}, bf16[64,256]{1,0:T(8,128)(2,1)}, u32[]{:S(2)}, u32[]{:S(2)}) collective-permute-start(bf16[64,256]{1,0:T(8,128)(2,1)S(1)} %fusion.44), channel_id=1, source_target_pairs={{16,0},{20,4},{24,8},{28,12},{32,16},{36,20},{40,24},{44,28},{48,3... | collective-permute-start | bytes 98312 | tf_op jit(solution)/shard_map/ppermute | solution.py:18
  77.4 24.9 %collective-permute-start.20 = (bf16[64,256]{1,0:T(8,128)(2,1)S(1)}, bf16[64,256]{1,0:T(8,128)(2,1)S(1)}, u32[]{:S(2)}, u32[]{:S(2)}) collective-permute-start(bf16[64,256]{1,0:T(8,128)(2,1)S(1)} %fusion.45), channel_id=1, source_target_pairs={{0,48},{4,52},{8,56},{12,60},{16,64},{20,68},{24,72},{28,76},{32,8... | collective-permute-start | bytes 98312 | tf_op jit(solution)/shard_map/ppermute | solution.py:18
  85.0 18.8 %collective-permute-start.19 = (bf16[64,256]{1,0:T(8,128)(2,1)S(1)}, bf16[64,256]{1,0:T(8,128)(2,1)S(1)}, u32[]{:S(2)}, u32[]{:S(2)}) collective-permute-start(bf16[64,256]{1,0:T(8,128)(2,1)S(1)} %fusion.45), channel_id=1, source_target_pairs={{48,0},{52,4},{56,8},{60,12},{64,16},{68,20},{72,24},{76,28},{80,3... | collective-permute-start | bytes 98312 | tf_op jit(solution)/shard_map/ppermute | solution.py:18
  86.5 7.5 %collective-permute-start.2 = (bf16[64,256]{1,0:T(8,128)(2,1)S(1)}, bf16[64,256]{1,0:T(8,128)(2,1)S(1)}, u32[]{:S(2)}, u32[]{:S(2)}) collective-permute-start(bf16[64,256]{1,0:T(8,128)(2,1)S(1)} %fusion.45), channel_id=1, source_target_pairs={{0,16},{16,0},{4,20},{20,4},{8,24},{24,8},{12,28},{28,12},{32,48},... | collective-permute-start | bytes 98312 | tf_op jit(solution)/shard_map/ppermute | solution.py:48
  94.0 22.2 %collective-permute-start.18 = (bf16[64,256]{1,0:T(8,128)(2,1)S(1)}, bf16[64,256]{1,0:T(8,128)(2,1)S(1)}, u32[]{:S(2)}, u32[]{:S(2)}) collective-permute-start(bf16[64,256]{1,0:T(8,128)(2,1)S(1)} %fusion.45), channel_id=1, source_target_pairs={{0,32},{4,36},{8,40},{12,44},{16,48},{20,52},{24,56},{28,60},{32,6... | collective-permute-start | bytes 98312 | tf_op jit(solution)/shard_map/ppermute | solution.py:18
  102.3 123.1 %collective-permute-start.17 = (bf16[64,256]{1,0:T(8,128)(2,1)S(1)}, bf16[64,256]{1,0:T(8,128)(2,1)}, u32[]{:S(2)}, u32[]{:S(2)}) collective-permute-start(bf16[64,256]{1,0:T(8,128)(2,1)S(1)} %fusion.45), channel_id=1, source_target_pairs={{32,0},{36,4},{40,8},{44,12},{48,16},{52,20},{56,24},{60,28},{64,3... | collective-permute-start | bytes 98312 | tf_op jit(solution)/shard_map/ppermute | solution.py:18
  103.8 21.0 %collective-permute-start.16 = (bf16[64,256]{1,0:T(8,128)(2,1)S(1)}, bf16[64,256]{1,0:T(8,128)(2,1)S(1)}, u32[]{:S(2)}, u32[]{:S(2)}) collective-permute-start(bf16[64,256]{1,0:T(8,128)(2,1)S(1)} %fusion.46), channel_id=1, source_target_pairs={{0,96},{4,100},{8,104},{12,108},{16,112},{20,116},{24,120},{28,124... | collective-permute-start | bytes 98312 | tf_op jit(solution)/shard_map/ppermute | solution.py:18
  116.2 7.0 %collective-permute-start.3 = (bf16[64,256]{1,0:T(8,128)(2,1)S(1)}, bf16[64,256]{1,0:T(8,128)(2,1)S(1)}, u32[]{:S(2)}, u32[]{:S(2)}) collective-permute-start(bf16[64,256]{1,0:T(8,128)(2,1)S(1)} %fusion.46), channel_id=1, source_target_pairs={{0,32},{32,0},{4,36},{36,4},{8,40},{40,8},{12,44},{44,12},{16,48},... | collective-permute-start | bytes 98312 | tf_op jit(solution)/shard_map/ppermute | solution.py:48
  123.2 7.6 %collective-permute-start.15 = (bf16[64,256]{1,0:T(8,128)(2,1)S(1)}, bf16[64,256]{1,0:T(8,128)(2,1)S(1)}, u32[]{:S(2)}, u32[]{:S(2)}) collective-permute-start(bf16[64,256]{1,0:T(8,128)(2,1)S(1)} %fusion.46), channel_id=1, source_target_pairs={{96,0},{100,4},{104,8},{108,12},{112,16},{116,20},{120,24},{124,28... | collective-permute-start | bytes 98312 | tf_op jit(solution)/shard_map/ppermute | solution.py:18
  124.8 7.4 %collective-permute-start.14 = (bf16[64,256]{1,0:T(8,128)(2,1)S(1)}, bf16[64,256]{1,0:T(8,128)(2,1)S(1)}, u32[]{:S(2)}, u32[]{:S(2)}) collective-permute-start(bf16[64,256]{1,0:T(8,128)(2,1)S(1)} %fusion.46), channel_id=1, source_target_pairs={{0,64},{4,68},{8,72},{12,76},{16,80},{20,84},{24,88},{28,92},{32,9... | collective-permute-start | bytes 98312 | tf_op jit(solution)/shard_map/ppermute | solution.py:18
  130.8 93.6 %collective-permute-start.13 = (bf16[64,256]{1,0:T(8,128)(2,1)S(1)}, bf16[64,256]{1,0:T(8,128)(2,1)}, u32[]{:S(2)}, u32[]{:S(2)}) collective-permute-start(bf16[64,256]{1,0:T(8,128)(2,1)S(1)} %fusion.46), channel_id=1, source_target_pairs={{64,0},{68,4},{72,8},{76,12},{80,16},{84,20},{88,24},{92,28},{96,3... | collective-permute-start | bytes 98312 | tf_op jit(solution)/shard_map/ppermute | solution.py:18
  132.2 9.8 %collective-permute-start.4 = (bf16[64,256]{1,0:T(8,128)(2,1)S(1)}, bf16[64,256]{1,0:T(8,128)(2,1)S(1)}, u32[]{:S(2)}, u32[]{:S(2)}) collective-permute-start(bf16[64,256]{1,0:T(8,128)(2,1)S(1)} %fusion.47), channel_id=1, source_target_pairs={{0,64},{64,0},{4,68},{68,4},{8,72},{72,8},{12,76},{76,12},{16,80},... | collective-permute-start | bytes 98312 | tf_op jit(solution)/shard_map/ppermute | solution.py:48
  142.1 11.4 %collective-permute-start.12 = (bf16[64,256]{1,0:T(8,128)(2,1)S(1)}, bf16[64,256]{1,0:T(8,128)(2,1)S(1)}, u32[]{:S(2)}, u32[]{:S(2)}) collective-permute-start(bf16[64,256]{1,0:T(8,128)(2,1)S(1)} %fusion.47), channel_id=1, source_target_pairs={{0,192},{4,196},{8,200},{12,204},{16,208},{20,212},{24,216},{28,22... | collective-permute-start | bytes 98312 | tf_op jit(solution)/shard_map/ppermute | solution.py:18
  153.5 11.8 %collective-permute-start.11 = (bf16[64,256]{1,0:T(8,128)(2,1)S(1)}, bf16[64,256]{1,0:T(8,128)(2,1)S(1)}, u32[]{:S(2)}, u32[]{:S(2)}) collective-permute-start(bf16[64,256]{1,0:T(8,128)(2,1)S(1)} %fusion.47), channel_id=1, source_target_pairs={{192,0},{196,4},{200,8},{204,12},{208,16},{212,20},{216,24},{220,2... | collective-permute-start | bytes 98312 | tf_op jit(solution)/shard_map/ppermute | solution.py:18
  165.3 7.8 %collective-permute-start.10 = (bf16[64,256]{1,0:T(8,128)(2,1)S(1)}, bf16[64,256]{1,0:T(8,128)(2,1)S(1)}, u32[]{:S(2)}, u32[]{:S(2)}) collective-permute-start(bf16[64,256]{1,0:T(8,128)(2,1)S(1)} %fusion.47), channel_id=1, source_target_pairs={{0,128},{4,132},{8,136},{12,140},{16,144},{20,148},{24,152},{28,15... | collective-permute-start | bytes 98312 | tf_op jit(solution)/shard_map/ppermute | solution.py:18
  173.2 13.3 %collective-permute-start.8 = (bf16[64,256]{1,0:T(8,128)(2,1)S(1)}, bf16[64,256]{1,0:T(8,128)(2,1)S(1)}, u32[]{:S(2)}, u32[]{:S(2)}) collective-permute-start(bf16[64,256]{1,0:T(8,128)(2,1)S(1)} %fusion.48), channel_id=1, source_target_pairs={{0,384},{4,388},{8,392},{12,396},{16,400},{20,404},{24,408},{28,41... | collective-permute-start | bytes 98312 | tf_op jit(solution)/shard_map/ppermute | solution.py:18
  186.5 9.7 %collective-permute-start.7 = (bf16[64,256]{1,0:T(8,128)(2,1)S(1)}, bf16[64,256]{1,0:T(8,128)(2,1)S(1)}, u32[]{:S(2)}, u32[]{:S(2)}) collective-permute-start(bf16[64,256]{1,0:T(8,128)(2,1)S(1)} %fusion.48), channel_id=1, source_target_pairs={{384,0},{388,4},{392,8},{396,12},{400,16},{404,20},{408,24},{412,2... | collective-permute-start | bytes 98312 | tf_op jit(solution)/shard_map/ppermute | solution.py:18
  196.2 2.9 %collective-permute-start.6 = (bf16[64,256]{1,0:T(8,128)(2,1)S(1)}, bf16[64,256]{1,0:T(8,128)(2,1)S(1)}, u32[]{:S(2)}, u32[]{:S(2)}) collective-permute-start(bf16[64,256]{1,0:T(8,128)(2,1)S(1)} %fusion.48), channel_id=1, source_target_pairs={{0,256},{4,260},{8,264},{12,268},{16,272},{20,276},{24,280},{28,28... | collective-permute-start | bytes 98312 | tf_op jit(solution)/shard_map/ppermute | solution.py:18
  199.0 14.5 %collective-permute-start.5 = (bf16[64,256]{1,0:T(8,128)(2,1)S(1)}, bf16[64,256]{1,0:T(8,128)(2,1)S(1)}, u32[]{:S(2)}, u32[]{:S(2)}) collective-permute-start(bf16[64,256]{1,0:T(8,128)(2,1)S(1)} %fusion.48), channel_id=1, source_target_pairs={{256,0},{260,4},{264,8},{268,12},{272,16},{276,20},{280,24},{284,2... | collective-permute-start | bytes 98312 | tf_op jit(solution)/shard_map/ppermute | solution.py:18
  213.5 1.3 copy-start.5
  213.5 9.8 %collective-permute-start.9 = (bf16[64,256]{1,0:T(8,128)(2,1)S(1)}, bf16[64,256]{1,0:T(8,128)(2,1)}, u32[]{:S(2)}, u32[]{:S(2)}) collective-permute-start(bf16[64,256]{1,0:T(8,128)(2,1)S(1)} %fusion.47), channel_id=1, source_target_pairs={{128,0},{132,4},{136,8},{140,12},{144,16},{148,20},{152,24},{156,2... | collective-permute-start | bytes 98312 | tf_op jit(solution)/shard_map/ppermute | solution.py:18
  242.7 2.7 %copy-start.3 = (bf16[1,4,512,512]{3,2,1,0:T(8,128)(2,1)S(1)}, bf16[1,4,512,512]{3,2,1,0:T(8,128)(2,1)}, u32[]{:S(2)}) copy-start(bf16[1,4,512,512]{3,2,1,0:T(8,128)(2,1)} %param.18) | copy-start | bytes 6291460
Sparse Core Ops, SparseCore 0:
  46.1 48.9 all-gather.1
